TPU v7x, 32 devices: a whole 2x2x4 slice. The times are simulated.
32 devices in a mesh: ctx: 8 (over z, y), fsdp: 4 (over x, core).
Axes of the slice: x: 2, y: 2, z: 4, core: 2. Of those that a mesh axis runs over, the one named last changes fastest.
Arguments:
- tokens: bfloat16 [1024, 2048], P('ctx'), may hold values from -24 to 24
- positions: int32 [1024], replicated, may hold values from 0 to 1023, each once
- pulse_indicator: int32 [2, 1024, 2048], P(None, 'ctx'), may hold values 0 or 1
- norm_gain: float32 [2048], replicated, may hold values from 0.1 to 1.9
- in_weight: bfloat16 [2048, 3, 1024], P(None, None, 'fsdp'), may hold values from -0.375 to 0.375
- out_weight: bfloat16 [1024, 2048], P('fsdp'), may hold values from -0.1875 to 0.1875
- upstream: bfloat16 [1024, 2048], P('ctx'), may hold values from -6 to 6
Outputs:
- block_out: bfloat16 [1024, 2048], P('ctx', 'fsdp')
- token_grad: float32 [1024, 2048], P('ctx', 'fsdp')
- gain_grad: float32 [2048], P('fsdp')
- in_grad: float32 [2048, 3, 1024], P('ctx', None, 'fsdp')
- out_grad: float32 [2048, 1024], P('ctx', 'fsdp')
Inputs may be any that keep to these rules, and one draw needn't show every extreme that they name: `positions`: each position of the sequence appears once.
All inputs are finite; a program needn't handle non-finite values. No bound on the sum of `pulse_indicator` on one device may be relied on, other than what follows from the above.
Results may differ from a plain program's by a relative error of at most 0.004.
The roundings to bfloat16 on the way count: a program that leaves them out, or rounds other values in their place, can miss the bound.
Values may be sent and summed in bfloat16 or wider, within the bound.
No kernel may reach another device: no remote copies, remote signals or barrier semaphores. Data moves between devices by JAX's collectives and lax.ppermute only.
A program may use at most 192 MiB of HBM per device.

v0:
```python
import jax
import jax.numpy as jnp
from jax import lax
from jax.sharding import PartitionSpec as P

HEAD_DIM = 128
TIMESTEPS = 2
SOFT_CAP = 30.0
LEAK_RATE = 0.5
THRESHOLD = 1.0
SURROGATE_SLOPE = 4.0
EPSILON = 1e-05


def leaky_forward(tokens, pulse_indicator, norm_gain):
    values = tokens.astype(jnp.float32)
    inv_rms = lax.rsqrt(jnp.mean(values * values, axis=-1, keepdims=True) + EPSILON)
    normed = values * inv_rms
    current = normed * norm_gain
    neuron_voltage = current
    voltage_trace_record = []
    pulse_number_sum = jnp.zeros_like(current)
    for present_instant in range(TIMESTEPS):
        binary_pulses = pulse_indicator[present_instant].astype(jnp.float32)
        if present_instant > 0:
            neuron_voltage = (
                LEAK_RATE
                * neuron_voltage
                * (1.0 - pulse_indicator[present_instant - 1].astype(jnp.float32))
                + current
            )
        voltage_trace_record.append(neuron_voltage)
        pulse_number_sum = pulse_number_sum + binary_pulses * neuron_voltage
    return (
        inv_rms,
        normed,
        voltage_trace_record,
        (pulse_number_sum / TIMESTEPS).astype(jnp.bfloat16),
    )


def leaky_backward(grad_rate, pulse_indicator, voltage_trace_record):
    rescaled_logits = grad_rate / TIMESTEPS
    leaky_level_prior = jnp.zeros_like(rescaled_logits)
    grad_current = jnp.zeros_like(rescaled_logits)
    for present_instant in reversed(range(TIMESTEPS)):
        binary_pulses = pulse_indicator[present_instant].astype(jnp.float32)
        capped_logits = jax.nn.sigmoid(
            SURROGATE_SLOPE * (voltage_trace_record[present_instant] - THRESHOLD)
        )
        voltage_adjoint = (
            rescaled_logits
            * (
                binary_pulses
                + voltage_trace_record[present_instant]
                * SURROGATE_SLOPE
                * capped_logits
                * (1.0 - capped_logits)
            )
            + leaky_level_prior
        )
        grad_current = grad_current + voltage_adjoint
        if present_instant > 0:
            leaky_level_prior = (
                LEAK_RATE
                * voltage_adjoint
                * (1.0 - pulse_indicator[present_instant - 1].astype(jnp.float32))
            )
    return grad_current


def body(tokens, positions, pulse_indicator, norm_gain, in_weight, out_weight, upstream):
    ctx_rank = lax.axis_index("ctx")
    fsdp_rank = lax.axis_index("fsdp")
    rows_here = tokens.shape[0]
    model_width = tokens.shape[1]
    share_cols = model_width // lax.axis_size("fsdp")
    local_width = out_weight.shape[0]
    heads_here = local_width // HEAD_DIM
    score_scale = HEAD_DIM ** (-0.5)
    own_pos = lax.dynamic_slice_in_dim(positions, ctx_rank * rows_here, rows_here)
    inv_rms, normed, voltage_trace_record, spikes = leaky_forward(
        tokens, pulse_indicator, norm_gain
    )
    flat_in = in_weight.reshape(model_width, 3 * local_width)
    project = jnp.dot(spikes, flat_in, preferred_element_type=jnp.float32).astype(jnp.bfloat16)
    project = project.reshape(rows_here, 3, local_width)
    query_flat = project[:, 0]
    queries = query_flat.reshape(rows_here, heads_here, HEAD_DIM)
    gathered = lax.all_gather(project[:, 1:], "ctx", axis=0, tiled=True)
    keys_all = gathered[:, 0].reshape(-1, heads_here, HEAD_DIM)
    values_all = gathered[:, 1].reshape(-1, heads_here, HEAD_DIM)
    allowed = positions[None, :] <= own_pos[:, None]
    scores = (
        jnp.einsum("rhd,khd->hrk", queries, keys_all, preferred_element_type=jnp.float32)
        * score_scale
    )
    squashed = jnp.tanh(scores / SOFT_CAP)
    exponent = jnp.where(allowed[None], jnp.exp(SOFT_CAP * squashed), 0.0)
    totals = jnp.sum(exponent, axis=-1, keepdims=True)
    attn_prob = exponent / totals
    prob_low = attn_prob.astype(jnp.bfloat16)
    attended = jnp.einsum("hrk,khd->rhd", prob_low, values_all, preferred_element_type=jnp.float32)
    attended = attended.astype(jnp.bfloat16).reshape(rows_here, local_width)
    partial_out = jnp.dot(attended, out_weight, preferred_element_type=jnp.float32)
    summed_out = lax.psum_scatter(partial_out, "fsdp", scatter_dimension=1, tiled=True)
    low_col = fsdp_rank * share_cols
    token_share = lax.dynamic_slice_in_dim(tokens, low_col, share_cols, 1).astype(jnp.float32)
    block_out = (token_share + summed_out).astype(jnp.bfloat16)
    grad_attn = jnp.dot(upstream, out_weight.T, preferred_element_type=jnp.float32).astype(
        jnp.bfloat16
    )
    grad_heads = grad_attn.reshape(rows_here, heads_here, HEAD_DIM)
    grad_prob = jnp.einsum(
        "rhd,khd->hrk", grad_heads, values_all, preferred_element_type=jnp.float32
    )
    delta = jnp.sum(attn_prob * grad_prob, axis=-1, keepdims=True)
    score_grad = (
        attn_prob * (grad_prob - delta) * (1.0 - squashed * squashed) * score_scale
    ).astype(jnp.bfloat16)
    grad_query = jnp.einsum(
        "hrk,khd->rhd", score_grad, keys_all, preferred_element_type=jnp.float32
    )
    grad_query = grad_query.astype(jnp.bfloat16).reshape(rows_here, local_width)
    grad_keys = jnp.einsum("hrk,rhd->khd", score_grad, queries, preferred_element_type=jnp.float32)
    grad_values = jnp.einsum(
        "hrk,rhd->khd", prob_low, grad_heads, preferred_element_type=jnp.float32
    )
    key_grads = lax.psum_scatter(
        jnp.stack(
            [
                grad_keys.reshape(rows_here * lax.axis_size("ctx"), local_width),
                grad_values.reshape(rows_here * lax.axis_size("ctx"), local_width),
            ],
            axis=1,
        ),
        "ctx",
        scatter_dimension=0,
        tiled=True,
    )
    grad_project = jnp.concatenate([grad_query[:, None], key_grads.astype(jnp.bfloat16)], axis=1)
    flat_grad = grad_project.reshape(rows_here, 3 * local_width)
    spike_part = jnp.dot(flat_grad, flat_in.T, preferred_element_type=jnp.float32)
    grad_spikes = lax.psum(spike_part, "fsdp")
    grad_current = leaky_backward(grad_spikes, pulse_indicator, voltage_trace_record)
    scaled_grad = grad_current * norm_gain
    row_mean = jnp.mean(scaled_grad * normed, axis=-1, keepdims=True)
    full_grad = upstream.astype(jnp.float32) + inv_rms * (scaled_grad - normed * row_mean)
    token_grad = lax.dynamic_slice_in_dim(full_grad, low_col, share_cols, 1)
    gain_part = lax.dynamic_slice_in_dim(
        jnp.sum(grad_current * normed, axis=0), low_col, share_cols
    )
    gain_grad = lax.psum(gain_part, "ctx")
    grad_inward = jnp.einsum("rc,rk->ck", spikes, flat_grad, preferred_element_type=jnp.float32)
    grad_outward = jnp.einsum("rc,rk->ck", upstream, attended, preferred_element_type=jnp.float32)
    weight_rows = lax.psum_scatter(
        jnp.concatenate([grad_inward, grad_outward], axis=1), "ctx", scatter_dimension=0, tiled=True
    )
    in_grad = weight_rows[:, : 3 * local_width].reshape(-1, 3, local_width)
    out_grad = weight_rows[:, 3 * local_width :]
    return (block_out, token_grad, gain_grad, in_grad, out_grad)


def solution(mesh):
    placed = (
        P("ctx", None),
        P(),
        P(None, "ctx", None),
        P(),
        P(None, None, "fsdp"),
        P("fsdp", None),
        P("ctx", None),
    )
    return jax.shard_map(
        body,
        mesh=mesh,
        in_specs=placed,
        out_specs=(
            P("ctx", "fsdp"),
            P("ctx", "fsdp"),
            P("fsdp"),
            P("ctx", None, "fsdp"),
            P("ctx", "fsdp"),
        ),
        check_vma=False,
    )
```

profile of v0, /device:TPU:0, one launch (start us, length us, event | category | flops | bytes accessed | tf_op | source)
XLA Modules:
  0.0 375.2 jit_solution(12632375523382011827)
XLA Ops:
  7.2 1.3 fusion.7
  8.6 4.9 %copy.23 = bf16[2048,3,256]{0,2,1:T(8,128)(2,1)} copy(bf16[2048,3,256]{2,0,1:T(8,128)(2,1)} %param.11) | data formatting | bytes 6291456 | tf_op args[4]
  13.4 2.7 convert_multiply_fusion
  16.1 0.8 copy-done.3
  16.9 1.2 convolution_convert_fusion
  18.1 0.2 copy.24
  18.3 0.7 slice.36
  19.0 0.0 reduce-scatter.6.cloned.1.call-start
  19.1 1.5 convolution_convert_fusion.2
  20.6 0.1 copy.39
  20.7 0.1 dynamic_slice.13
  20.8 0.1 broadcast_compare_fusion
  21.0 40.4 %all-gather.2.cloned.1.call-done = bf16[1024,2,256]{0,2,1:T(8,128)(2,1)} async-done(((bf16[128,2,256]{0,2,1:T(8,128)(2,1)}), bf16[1024,2,256]{0,2,1:T(8,128)(2,1)}) %all-gather.2.cloned.1.call-update) | async-done | bytes 1048592 | tf_op jit(solution)/shard_map/all_gather | solution.py:90
  61.4 1.3 fusion.44
  62.7 0.8 copy-done.4
  63.4 1.3 fusion.46
  64.8 0.6 fusion.22
  65.4 1.0 copy-done.8
  66.4 1.5 fusion.29
  67.9 4.2 %fusion.17 = f32[2,128,1024]{2,1,0:T(8,128)} fusion(bf16[128,2,128]{0,2,1:T(8,128)(2,1)S(1)} %bitcast.88, f32[2,128,1024]{2,1,0:T(8,128)} %fusion.46, f32[2,128,1024]{2,1,0:T(8,128)} %copy-done.8, f32[2,128]{1,0:T(2,128)S(1)} %get-tuple-element.22, pred[128,1024]{1,0:T(8,128)(4,1)S(1)} %broadcast_compare_fusion), kind=kOutput, calls=%fused_computation.37 | convolution fusion | flops 70780160 | bytes 3343360 | tf_op jit(solution)/shard_map/hrk,rhd->khd/dot_general | solution.py:125
  72.2 2.5 copy.31
  74.7 2.6 copy.30
  77.3 3.0 pad_maximum_fusion.1
  80.3 0.0 reduce-scatter.4.cloned.1.call-start
  80.4 1.8 convolution_convert_fusion.3
  82.2 1.3 fusion.45
  83.6 0.0 all-reduce.2.cloned.1.call-start
  83.6 3.4 convolution_convert_fusion.1
  87.0 0.1 copy.32
  87.1 2.9 convolution_bitcast_fusion
  89.9 57.2 %reduce-scatter.6.cloned.1.call-done = f32[128,2,256]{2,0,1:T(8,128)} async-done(((f32[1024,2,256]{2,0,1:T(8,128)}), f32[128,2,256]{2,0,1:T(8,128)}) %reduce-scatter.6.cloned.1.call-update) | async-done | bytes 262160 | tf_op jit(solution)/shard_map/reduce_scatter | solution.py:129
  147.2 1.0 convert_element_type.75
  148.1 0.7 pad_maximum_fusion.2
  148.8 1.1 copy.33
  149.9 4.0 %convolution_bitcast_fusion.1 = f32[128,2048]{1,0:T(8,128)} fusion(bf16[2048,3,256]{2,0,1:T(8,128)(2,1)} %param.11, bf16[128,2,256]{2,0,1:T(8,128)(2,1)S(1)} %convert_element_type.75, bf16[128,1,256]{2,0,1:T(8,128)(2,1)S(1)} %copy.32), kind=kOutput, calls=%fused_computation.3 | convolution fusion | flops 402751488 | bytes 4390912 | tf_op jit(solution)/shard_map/dot_general | solution.py:143
  154.0 2.0 fusion.47
  156.0 6.2 %pad_maximum_fusion = f32[2048,1024]{0,1:T(8,128)} fusion(f32[2048,256]{0,1:T(8,128)} %convolution_bitcast_fusion, f32[2048,768]{0,1:T(8,128)S(1)} %fusion.47), kind=kLoop, calls=%fused_computation.1 | loop fusion | flops 2097152 | bytes 16777216 | tf_op jit(solution)/shard_map/concatenate | solution.py:157
  162.2 11.4 %reduce-scatter.4.cloned.1.call-done = f32[128,512]{1,0:T(8,128)} async-done(((f32[128,2048]{1,0:T(8,128)}), f32[128,512]{1,0:T(8,128)}) %reduce-scatter.4.cloned.1.call-update) | async-done | bytes 262160 | tf_op jit(solution)/shard_map/reduce_scatter | solution.py:106
  173.6 1.7 add_convert_fusion
  175.3 36.8 %all-reduce.2.cloned.1.call-done = f32[128,2048]{1,0:T(8,128)} async-done(((f32[128,2048]{1,0:T(8,128)}), f32[128,2048]{1,0:T(8,128)}) %all-reduce.2.cloned.1.call-update) | async-done | bytes 1048592 | tf_op jit(solution)/shard_map/psum | solution.py:144
  212.1 3.9 %multiply_reduce_fusion = (f32[2048]{0:T(1024)S(1)}, f32[128]{0:T(128)S(1)}, f32[128,2048]{1,0:T(8,128)}) fusion(bf16[128,2048]{1,0:T(8,128)(2,1)} %param.7, f32[128]{0:T(128)S(1)} %add_rsqrt_fusion, f32[2048]{0:T(1024)S(1)} %copy-done.6, s32[2,128,2048]{2,1,0:T(8,128)S(1)} %copy-done.2, f32[128,2048]{1,0:T(8,128)} %all-reduce.2.cloned.1.call-done), kind=kLoop, calls=%fused_computation.31 | loop fusion | flops 10745728 | bytes 4736000 | tf_op jit(solution)/shard_map/reduce_sum | solution.py:151
  216.0 0.1 dynamic_slice.15
  216.1 22.3 %psum.15 = f32[512]{0:T(512)} all-reduce(f32[512]{0:T(512)S(1)} %dynamic_slice.15), channel_id=1, replica_groups=mesh['ctx'=8,'fsdp'=4] {'ctx'}, use_global_device_ids=true, to_apply=%region_8.9 | all-reduce | flops 512 | bytes 4096 | tf_op jit(solution)/shard_map/psum | solution.py:153
  238.4 1.9 fusion.28
  240.3 125.2 %reduce-scatter.8.cloned.1.call-done = f32[256,1024]{0,1:T(8,128)} async-done(((f32[2048,1024]{0,1:T(8,128)}), f32[256,1024]{0,1:T(8,128)}) %reduce-scatter.8.cloned.1.call-update) | async-done | bytes 1048592 | tf_op jit(solution)/shard_map/reduce_scatter | solution.py:156
  365.5 1.2 slice.40
  366.7 1.1 copy.34
  367.9 0.8 copy.35
  (27 shorter events, 0.2 us)
Async XLA Ops:
  7.2 11.9 %copy-start = (bf16[256,2048]{1,0:T(8,128)(2,1)S(1)}, bf16[256,2048]{1,0:T(8,128)(2,1)}, u32[]{:S(2)}) copy-start(bf16[256,2048]{1,0:T(8,128)(2,1)} %param.12) | copy-start | bytes 3145732
  7.2 54.2 %all-gather.2.cloned.1.call-start = ((), (), s32[]{:S(2)}) async-start(), calls=%async_computation.3 | async-start | bytes 1179648 | tf_op jit(solution)/shard_map/all_gather | solution.py:90
  8.5 4.9 %copy-start.2 = (s32[2,128,2048]{2,1,0:T(8,128)S(1)}, s32[2,128,2048]{2,1,0:T(8,128)}, u32[]{:S(2)}) copy-start(s32[2,128,2048]{2,1,0:T(8,128)} %param.9) | copy-start | bytes 6291460
  8.6 4.9 %copy-start.6 = (f32[2048]{0:T(1024)S(1)}, f32[2048]{0:T(1024)}, u32[]{:S(2)}) copy-start(f32[2048]{0:T(1024)} %param.10) | copy-start | bytes 24580
  13.4 3.5 copy-start.1
  16.1 0.8 copy-start.3
  16.9 3.8 %copy-start.7 = (s32[1024]{0:T(1024)S(1)}, s32[1024]{0:T(1024)}, u32[]{:S(2)}) copy-start(s32[1024]{0:T(1024)} %param.8) | copy-start | bytes 12292
  19.0 128.2 %reduce-scatter.6.cloned.1.call-start = ((), (), s32[]{:S(2)}) async-start(), calls=%async_computation.5 | async-start | bytes 2359296 | tf_op jit(solution)/shard_map/reduce_scatter | solution.py:129
  62.6 0.8 copy-start.4
  62.7 2.1 copy-start.5
  65.4 1.0 copy-start.8
  80.3 93.3 %reduce-scatter.4.cloned.1.call-start = ((), (), s32[]{:S(2)}) async-start(), calls=%async_computation.4 | async-start | bytes 1310720 | tf_op jit(solution)/shard_map/reduce_scatter | solution.py:106
  83.6 128.5 %all-reduce.2.cloned.1.call-start = ((), (), s32[]{:S(2)}) async-start(), calls=%async_computation.6 | async-start | bytes 2097152 | tf_op jit(solution)/shard_map/psum | solution.py:144
  153.9 211.6 %reduce-scatter.8.cloned.1.call-start = ((), (), s32[]{:S(2)}) async-start(), calls=%async_computation.7 | async-start | bytes 9437184 | tf_op jit(solution)/shard_map/reduce_scatter | solution.py:156
  365.5 2.4 slice-start
Sparse Core Ops, SparseCore 0:
  19.1 42.2 all-gather.1
  80.4 66.6 reduce-scatter.5
  149.7 23.8 reduce-scatter.3
  176.0 36.0 all-reduce.1
  215.6 149.8 reduce-scatter.7
where the time goes:
time: 376 us; the launch traced here: 375 us
  waiting for transfers between devices  271 us (72%)
  matrix products  25.8 us (7%)
  other arithmetic  22.5 us (6%)
  blocking collectives  22.3 us (6%)
  local copies, waits for them, and re-layouts  19.3 us (5%)
  between operations  14 us (4%)
    reduce_scatter x1, waiting for transfers between devices, body(): lax.psum_scatter(jnp.concatenate([grad_inward, grad_outward], axis=1), 'c...  125 us
    reduce_scatter x1, waiting for transfers between devices, body(): lax.psum_scatter(jnp.stack([grad_keys.reshape(rows_here * lax.axis_size('...  57.2 us
    all_gather x1, waiting for transfers between devices, body(): gathered = lax.all_gather(project[:, 1:], 'ctx', axis=0, tiled=True)  40.4 us
    psum x1, waiting for transfers between devices, body(): grad_spikes = lax.psum(spike_part, 'fsdp')  36.8 us
    psum x1, blocking collectives, body(): gain_grad = lax.psum(gain_part, 'ctx')  22.3 us
    reduce_scatter x1, waiting for transfers between devices, body(): lax.psum_scatter(partial_out, 'fsdp', scatter_dimension=1, tiled=True)  11.4 us
    unnamed x21, local copies, waits for them, and re-layouts  9.44 us
  transfers between devices with their start and end apart: 5, of which 5 were waited for; matrix products, arithmetic and copies ran while one was open for 9% of the time, Pallas kernels for 0%

commit v1 on v0

--- a/solution.py
+++ b/solution.py
@@ -10,6 +10,14 @@
 THRESHOLD = 1.0
 SURROGATE_SLOPE = 4.0
 EPSILON = 1e-05
+
+
+def gather_from_all(value, axis, dim):
+    devices = lax.axis_size(axis)
+    repeats = [devices if d == dim else 1 for d in range(value.ndim)]
+    return lax.all_to_all(
+        jnp.tile(value, repeats), axis, split_axis=dim, concat_axis=dim, tiled=True
+    )
 
 
 def leaky_forward(tokens, pulse_indicator, norm_gain):
@@ -87,7 +95,7 @@
     project = project.reshape(rows_here, 3, local_width)
     query_flat = project[:, 0]
     queries = query_flat.reshape(rows_here, heads_here, HEAD_DIM)
-    gathered = lax.all_gather(project[:, 1:], "ctx", axis=0, tiled=True)
+    gathered = gather_from_all(project[:, 1:], "ctx", 0)
     keys_all = gathered[:, 0].reshape(-1, heads_here, HEAD_DIM)
     values_all = gathered[:, 1].reshape(-1, heads_here, HEAD_DIM)
     allowed = positions[None, :] <= own_pos[:, None]

time: 376 us -> 369 us (0.981)
  waiting for transfers between devices: 271 us -> 259 us
  starting transfers between devices: 0.21 us -> 7.62 us
  local copies, waits for them, and re-layouts: 19.3 us -> 23.5 us
    all_gather x1 -> x0, waiting for transfers between devices: 40.4 us -> none  [body(): gathered = lax.all_gather(project[:, 1:], 'ctx', axis=0, tiled=True)]
    all_to_all x0 -> x1, waiting for transfers between devices: none -> 24.8 us  [gather_from_all(): lax.all_to_all(jnp.tile(value, repeats), axis, split_axis=dim, concat_axi...]
    all_to_all x0 -> x1, starting transfers between devices: none -> 7.28 us  [gather_from_all(): lax.all_to_all(jnp.tile(value, repeats), axis, split_axis=dim, concat_axi...]
    unnamed x21 -> x28, local copies, waits for them, and re-layouts: 9.44 us -> 12.2 us
  transfers between devices with their start and end apart: 5 -> 5, of which waited for: 5 -> 5; matrix products, arithmetic and copies ran while one was open for 9% -> 8% of each run, Pallas kernels for 0% -> 0%
where the time goes in v1:
time: 369 us
  waiting for transfers between devices  259 us (70%)
  local copies, waits for them, and re-layouts  23.5 us (6%)
  matrix products  23.1 us (6%)
  blocking collectives  22.4 us (6%)
  other arithmetic  19.2 us (5%)
  between operations  14 us (4%)
  starting transfers between devices  7.62 us (2%)
    reduce_scatter x1, waiting for transfers between devices, body(): lax.psum_scatter(jnp.concatenate([grad_inward, grad_outward], axis=1), 'c...  125 us
    reduce_scatter x1, waiting for transfers between devices, body(): lax.psum_scatter(jnp.stack([grad_keys.reshape(rows_here * lax.axis_size('...  58.8 us
    psum x1, waiting for transfers between devices, body(): grad_spikes = lax.psum(spike_part, 'fsdp')  36.9 us
    all_to_all x1, waiting for transfers between devices, gather_from_all(): lax.all_to_all(jnp.tile(value, repeats), axis, split_axis=dim, concat_axi...  24.8 us
    psum x1, blocking collectives, body(): gain_grad = lax.psum(gain_part, 'ctx')  22.4 us
    reduce_scatter x1, waiting for transfers between devices, body(): lax.psum_scatter(partial_out, 'fsdp', scatter_dimension=1, tiled=True)  13.1 us
    unnamed x28, local copies, waits for them, and re-layouts  12.2 us
  transfers between devices with their start and end apart: 5, of which 5 were waited for; matrix products, arithmetic and copies ran while one was open for 8% of the time, Pallas kernels for 0%

profile of v1, /device:TPU:0, one launch (start us, length us, event | category | flops | bytes accessed | tf_op | source)
XLA Modules:
  0.0 368.6 jit_solution(6875663364809647980)
XLA Ops:
  7.2 1.3 fusion.7
  8.5 4.9 %copy.36 = bf16[2048,3,256]{0,2,1:T(8,128)(2,1)} copy(bf16[2048,3,256]{2,0,1:T(8,128)(2,1)} %param.11) | data formatting | bytes 6291456 | tf_op args[4]
  13.4 2.8 convert_multiply_fusion
  16.2 0.8 copy-done.4
  17.0 1.2 convolution_convert_fusion
  18.2 0.2 copy.37
  18.4 0.1 copy.38
  18.5 1.5 tile.4
  20.1 7.3 %all-to-all-start = ((bf16[1024,2,256]{2,1,0:T(2,128)(2,1)}), bf16[1024,2,256]{2,1,0:T(2,128)(2,1)S(1)}, u32[]{:S(2)}, u32[]{:S(2)}) async-start(bf16[1024,2,256]{2,1,0:T(2,128)(2,1)} %bitcast.4), calls=%async_computation | async-start | bytes 2097152 | tf_op jit(solution)/shard_map/all_to_all | solution.py:18
  27.4 0.5 convolution_convert_fusion.2
  27.9 0.1 copy.56
  28.1 0.1 dynamic_slice.13
  28.1 0.1 broadcast_compare_fusion
  28.3 24.8 %all-to-all-done = bf16[1024,2,256]{2,1,0:T(2,128)(2,1)S(1)} async-done(((bf16[1024,2,256]{2,1,0:T(2,128)(2,1)}), bf16[1024,2,256]{2,1,0:T(2,128)(2,1)S(1)}, u32[]{:S(2)}, u32[]{:S(2)}) %all-to-all-start) | async-done | bytes 1048608 | tf_op jit(solution)/shard_map/all_to_all | solution.py:18
  53.1 2.3 fusion.44
  55.4 3.5 copy.55
  58.9 1.3 copy.39
  60.2 0.3 fusion.46
  60.6 2.0 fusion.22
  62.7 1.0 copy-done.11
  63.6 1.5 fusion.29
  65.1 3.7 fusion.17
  68.8 1.6 copy.47
  70.4 1.6 copy.46
  71.9 1.5 pad_maximum_fusion.1
  73.5 1.9 convolution_convert_fusion.3
  75.4 1.3 fusion.45
  76.8 3.2 convolution_convert_fusion.1
  80.0 0.1 copy.48
  80.1 1.5 convolution_bitcast_fusion
  81.6 58.8 %reduce-scatter.6.cloned.1.call-done = f32[128,2,256]{2,0,1:T(8,128)} async-done(((f32[1024,2,256]{2,0,1:T(8,128)}), f32[128,2,256]{2,0,1:T(8,128)}) %reduce-scatter.6.cloned.1.call-update) | async-done | bytes 262160 | tf_op jit(solution)/shard_map/reduce_scatter | solution.py:137
  140.4 1.0 convert_element_type.75
  141.3 0.7 pad_maximum_fusion.2
  142.0 1.1 copy.49
  143.1 4.1 %convolution_bitcast_fusion.1 = f32[128,2048]{1,0:T(8,128)} fusion(bf16[2048,3,256]{2,0,1:T(8,128)(2,1)} %param.11, bf16[128,2,256]{2,0,1:T(8,128)(2,1)S(1)} %convert_element_type.75, bf16[128,1,256]{2,0,1:T(8,128)(2,1)S(1)} %copy.48), kind=kOutput, calls=%fused_computation.3 | convolution fusion | flops 402751488 | bytes 4390912 | tf_op jit(solution)/shard_map/dot_general | solution.py:151
  147.2 0.2 reduce-scatter.8.cloned.1.call-start
  147.4 2.0 fusion.47
  149.4 4.3 %pad_maximum_fusion = f32[2048,1024]{0,1:T(8,128)} fusion(f32[2048,256]{0,1:T(8,128)S(1)} %convolution_bitcast_fusion, f32[2048,768]{0,1:T(8,128)S(1)} %fusion.47), kind=kLoop, calls=%fused_computation.1 | loop fusion | flops 2097152 | bytes 16777216 | tf_op jit(solution)/shard_map/concatenate | solution.py:165
  153.7 13.1 %reduce-scatter.4.cloned.1.call-done = f32[128,512]{1,0:T(8,128)} async-done(((f32[128,2048]{1,0:T(8,128)}), f32[128,512]{1,0:T(8,128)}) %reduce-scatter.4.cloned.1.call-update) | async-done | bytes 262160 | tf_op jit(solution)/shard_map/reduce_scatter | solution.py:114
  166.8 1.7 add_convert_fusion
  168.5 36.9 %all-reduce.2.cloned.1.call-done = f32[128,2048]{1,0:T(8,128)} async-done(((f32[128,2048]{1,0:T(8,128)}), f32[128,2048]{1,0:T(8,128)}) %all-reduce.2.cloned.1.call-update) | async-done | bytes 1048592 | tf_op jit(solution)/shard_map/psum | solution.py:152
  205.4 3.9 %multiply_reduce_fusion = (f32[2048]{0:T(1024)S(1)}, f32[128]{0:T(128)S(1)}, f32[128,2048]{1,0:T(8,128)}) fusion(bf16[128,2048]{1,0:T(8,128)(2,1)} %param.7, f32[128]{0:T(128)S(1)} %add_rsqrt_fusion, f32[2048]{0:T(1024)S(1)} %copy-done.9, s32[2,128,2048]{2,1,0:T(8,128)S(1)} %copy-done.3, f32[128,2048]{1,0:T(8,128)} %all-reduce.2.cloned.1.call-done), kind=kLoop, calls=%fused_computation.31 | loop fusion | flops 10745728 | bytes 4736000 | tf_op jit(solution)/shard_map/reduce_sum | solution.py:159
  209.4 22.4 %psum.15 = f32[512]{0:T(512)} all-reduce(f32[512]{0:T(512)S(1)} %dynamic_slice.15), channel_id=1, replica_groups=mesh['ctx'=8,'fsdp'=4] {'ctx'}, use_global_device_ids=true, to_apply=%region_8.9 | all-reduce | flops 512 | bytes 4096 | tf_op jit(solution)/shard_map/psum | solution.py:161
  231.9 1.9 fusion.28
  233.8 125.0 %reduce-scatter.8.cloned.1.call-done = f32[256,1024]{0,1:T(8,128)} async-done(((f32[2048,1024]{0,1:T(8,128)}), f32[256,1024]{0,1:T(8,128)}) %reduce-scatter.8.cloned.1.call-update) | async-done | bytes 1048592 | tf_op jit(solution)/shard_map/reduce_scatter | solution.py:164
  358.8 1.2 slice.40
  360.1 1.1 copy.50
  361.2 0.8 copy.51
  (36 shorter events, 0.3 us)
Async XLA Ops:
  7.2 20.3 %copy-start = (bf16[256,2048]{1,0:T(8,128)(2,1)S(1)}, bf16[256,2048]{1,0:T(8,128)(2,1)}, u32[]{:S(2)}) copy-start(bf16[256,2048]{1,0:T(8,128)(2,1)} %param.12) | copy-start | bytes 3145732
  8.5 4.9 %copy-start.2 = (s32[2,128,2048]{2,1,0:T(8,128)S(1)}, s32[2,128,2048]{2,1,0:T(8,128)}, u32[]{:S(2)}) copy-start(s32[2,128,2048]{2,1,0:T(8,128)} %param.9) | copy-start | bytes 6291460
  8.5 4.9 %copy-start.9 = (f32[2048]{0:T(1024)S(1)}, f32[2048]{0:T(1024)}, u32[]{:S(2)}) copy-start(f32[2048]{0:T(1024)} %param.10) | copy-start | bytes 24580
  13.4 3.6 copy-start.1
  16.2 0.8 copy-start.4
  17.0 10.4 %copy-start.5 = (bf16[128,2048]{1,0:T(8,128)(2,1)S(1)}, bf16[128,2048]{1,0:T(8,128)(2,1)}, u32[]{:S(2)}) copy-start(bf16[128,2048]{1,0:T(8,128)(2,1)} %param.13) | copy-start | bytes 1572868
  18.2 9.9 %copy-start.10 = (s32[1024]{0:T(1024)S(1)}, s32[1024]{0:T(1024)}, u32[]{:S(2)}) copy-start(s32[1024]{0:T(1024)} %param.8) | copy-start | bytes 12292
  20.1 33.0 %all-to-all-start = ((bf16[1024,2,256]{2,1,0:T(2,128)(2,1)}), bf16[1024,2,256]{2,1,0:T(2,128)(2,1)S(1)}, u32[]{:S(2)}, u32[]{:S(2)}) async-start(bf16[1024,2,256]{2,1,0:T(2,128)(2,1)} %bitcast.4), calls=%async_computation | async-start | bytes 2097152 | tf_op jit(solution)/shard_map/all_to_all | solution.py:18
  27.4 113.0 %reduce-scatter.6.cloned.1.call-start = ((), (), s32[]{:S(2)}) async-start(), calls=%async_computation.5 | async-start | bytes 2359296 | tf_op jit(solution)/shard_map/reduce_scatter | solution.py:137
  60.2 4.9 %copy-start.6 = (bf16[1024,1,256]{0,2,1:T(8,128)(2,1)}, bf16[1024,1,256]{0,2,1:T(8,128)(2,1)S(1)}, u32[]{:S(2)}) copy-start(bf16[1024,1,256]{0,2,1:T(8,128)(2,1)S(1)} %copy.39) | copy-start | bytes 1572868
  60.6 4.6 %copy-start.7 = (f32[2,128,1024]{2,1,0:T(8,128)}, f32[2,128,1024]{2,1,0:T(8,128)S(1)}, u32[]{:S(2)}) copy-start(f32[2,128,1024]{2,1,0:T(8,128)S(1)} %fusion.46) | copy-start | bytes 3145732
  62.7 1.0 copy-start.11
  73.4 3.3 copy-start.8
  73.5 93.4 %reduce-scatter.4.cloned.1.call-start = ((), (), s32[]{:S(2)}) async-start(), calls=%async_computation.4 | async-start | bytes 1310720 | tf_op jit(solution)/shard_map/reduce_scatter | solution.py:114
  76.7 128.7 %all-reduce.2.cloned.1.call-start = ((), (), s32[]{:S(2)}) async-start(), calls=%async_computation.6 | async-start | bytes 2097152 | tf_op jit(solution)/shard_map/psum | solution.py:152
  147.2 211.6 %reduce-scatter.8.cloned.1.call-start = ((), (), s32[]{:S(2)}) async-start(), calls=%async_computation.7 | async-start | bytes 9437184 | tf_op jit(solution)/shard_map/reduce_scatter | solution.py:164
  153.7 51.7 %copy-start.3 = (s32[2,128,2048]{2,1,0:T(8,128)S(1)}, s32[2,128,2048]{2,1,0:T(8,128)}, u32[]{:S(2)}) copy-start(s32[2,128,2048]{2,1,0:T(8,128)} %param.9) | copy-start | bytes 6291460
  358.8 2.4 slice-start
Sparse Core Ops, SparseCore 0:
  73.6 66.7 reduce-scatter.5
  142.9 23.9 reduce-scatter.3
  169.3 36.0 all-reduce.1
  208.9 149.8 reduce-scatter.7
